TPU v7x, 32 devices: a whole 2x2x4 slice. The times are simulated.
32 devices in a mesh: member: 2 (over x), blk: 8 (over z, y), feat: 2 (over core).
Axes of the slice: x: 2, y: 2, z: 4, core: 2. Of those that a mesh axis runs over, the one named last changes fastest.
Arguments:
- features: bfloat16 [256, 4096], P(('member', 'feat'), 'blk'), parts along dimension 0, may hold values from -6 to 6
- w_node: bfloat16 [4, 128, 128], P('member', None, 'feat'), parts along dimension 0, may hold values from -0.5 to 0.5
- w_msg: bfloat16 [4, 128, 128], P('member', None, 'feat'), parts along dimension 0, may hold values from -1.5 to 1.5
- w_mix: bfloat16 [4, 128, 128], P('member', 'feat'), parts along dimension 0, may hold values from -0.5 to 0.5
- hbias: float32 [4, 128], P('member', 'feat'), parts along dimension 0, may hold values from -3 to 3
- obias: float32 [4, 128], P('member', 'feat'), parts along dimension 0, may hold values from -3 to 3
- anchor_node: bfloat16 [4, 128, 128], P('member', None, 'feat'), parts along dimension 0, may hold values from -0.5 to 0.5
- anchor_msg: bfloat16 [4, 128, 128], P('member', None, 'feat'), parts along dimension 0, may hold values from -1.5 to 1.5
- anchor_mix: bfloat16 [4, 128, 128], P('member', 'feat'), parts along dimension 0, may hold values from -0.5 to 0.5
- cotangent: bfloat16 [256, 4096], P(('member', 'feat'), 'blk'), parts along dimension 0, may hold values from -0.09375 to 0.09375
- tile_cols: int32 [64, 12], P(('member', 'blk')), parts along dimension 0, may hold values from 0 to 31, as said below
- tile_count: int32 [64], P(('member', 'blk')), parts along dimension 0, may hold values from 3 to 12, as said below
- tile_masks: int32 [64, 12, 128, 128], P(('member', 'blk')), parts along dimension 0, may hold values 0 or 1
Outputs:
- out_features: bfloat16 [256, 4096], P(('member', 'feat'), 'blk'), parts along dimension 0
- grad_node: float32 [4, 128, 128], P('member', None, 'feat'), parts along dimension 0
- grad_msg: float32 [4, 128, 128], P('member', None, 'feat'), parts along dimension 0
- grad_mix: float32 [4, 128, 128], P('member', 'feat'), parts along dimension 0
- grad_hbias: float32 [4, 128], P('member', 'feat'), parts along dimension 0
- grad_obias: float32 [4, 128], P('member', 'feat'), parts along dimension 0
There are 2 independent parts, one for each index of `member`. A program takes and returns all parts, laid end to end along the dimension named above; each array names one. Nothing has to cross between parts.
Inputs may be any that keep to these rules, and one draw needn't show every extreme that they name: Only slots 0 to tile_count[r] - 1 of block row r are used; some block row has exactly 12 live slots. Slot 0 of every block row names the row's own block. For every slot of row r, the blk index holding the named block (tile_cols // 4) lies within 1 step of r // 4 around the closed cycle of 8 indices; slot 1 lies exactly 1 step ahead and slot 2 exactly 1 step behind in every row.
All inputs are finite; a program needn't handle non-finite values. No bound on the sum of `tile_masks` on one device may be relied on, other than what follows from the above.
Results may differ from a plain program's by a relative error of at most 0.01.
Values may be sent and summed in bfloat16 or wider, within the bound.
A program may use at most 64 MiB of HBM per device.

v0:
```python
import jax
import jax.numpy as jnp
from jax import lax
from jax.sharding import PartitionSpec as P


def shifted(value, axis, steps):
    count = lax.axis_size(axis)
    pairs = [(source, (source + steps) % count) for source in range(count)]
    return lax.ppermute(value, axis, pairs)


def mix_rows(weights, hidden):
    return jnp.einsum("hc,hn->cn", weights, hidden, preferred_element_type=jnp.float32)


def input_rows(combined, d_round, feat_half, row_count):
    width = combined.shape[0] // 2
    wanted = jnp.arange(row_count, dtype=jnp.int32)
    owner = wanted // (2 * feat_half)
    within = wanted % (2 * feat_half)
    source = jnp.where(
        within < feat_half,
        owner * feat_half + within,
        width + owner * feat_half + within - feat_half,
    )
    picked = jnp.take(combined, source, axis=0)
    return jnp.einsum("ch,hn->cn", picked, d_round, preferred_element_type=jnp.float32)


def local(
    features,
    w_node,
    w_msg,
    w_mix,
    hbias,
    obias,
    anchor_node,
    anchor_msg,
    anchor_mix,
    cotangent,
    tile_cols,
    tile_count,
    tile_masks,
):
    block_rows = tile_masks.shape[0]
    slot_count = tile_masks.shape[1]
    tile_size = tile_masks.shape[2]
    feat_half = features.shape[0]
    node_count = features.shape[1]
    layer_count = w_node.shape[0]
    cycle_size = lax.axis_size("blk")
    cycle_place = lax.axis_index("blk")
    reach_dev = max(1, cycle_size // 8)
    live_flags = (jnp.arange(slot_count, dtype=jnp.int32)[None, :] < tile_count[:, None]).astype(
        jnp.int32
    )
    live_masks = tile_masks * live_flags[:, :, None, None]
    degree = (1 + jnp.sum(live_masks, axis=(1, 3))).astype(jnp.float32).reshape(node_count)
    mask_values = live_masks.astype(jnp.bfloat16)
    column_dev = tile_cols // block_rows
    column_within = tile_cols % block_rows
    target = (column_dev - cycle_place + reach_dev) % cycle_size * block_rows + column_within
    window_blocks = (2 * reach_dev + 1) * block_rows
    acts = features
    saved = []
    for layer in range(layer_count):

        def step(carried, unused):
            below, above = carried
            below = shifted(below, "blk", 1)
            above = shifted(above, "blk", -1)
            return ((below, above), (below, above))

        unused_state, (lowers, uppers) = lax.scan(step, (acts, acts), None, length=reach_dev)
        window = jnp.concatenate([jnp.flip(lowers, 0), acts[None], uppers], axis=0)
        aggregate_window = jnp.moveaxis(window, 0, 1).reshape(feat_half, window_blocks, tile_size)
        chosen = jnp.take(aggregate_window, target, axis=1)
        summed = jnp.einsum(
            "fbkj,bkij->fbi", chosen, mask_values, preferred_element_type=jnp.float32
        )
        summed = summed.reshape(feat_half, node_count)
        message = ((acts.astype(jnp.float32) + summed) / degree[None, :]).astype(jnp.bfloat16)
        acts_all, message_all = (
            lax.all_gather(acts, "feat", axis=0, tiled=True),
            lax.all_gather(message, "feat", axis=0, tiled=True),
        )
        pre = (
            jnp.einsum("fh,fn->hn", w_node[layer], acts_all, preferred_element_type=jnp.float32)
            + jnp.einsum("fh,fn->hn", w_msg[layer], message_all, preferred_element_type=jnp.float32)
            + hbias[layer][:, None]
        )
        hidden = jax.nn.silu(pre).astype(jnp.bfloat16)
        mixed = lax.psum_scatter(
            mix_rows(w_mix[layer], hidden), "feat", scatter_dimension=0, tiled=True
        )
        output = (acts.astype(jnp.float32) + mixed + obias[layer][:, None]).astype(jnp.bfloat16)
        saved.append((acts_all, message_all, pre, hidden))
        acts = output
    grads_node = [None] * layer_count
    grads_msg = [None] * layer_count
    grads_mix = [None] * layer_count
    grads_hbias = [None] * layer_count
    grads_obias = [None] * layer_count
    d_out = cotangent
    for layer in range(layer_count - 1, -1, -1):
        acts_keep, message_keep, pre, hidden = saved[layer]
        local_obias = jnp.sum(d_out.astype(jnp.float32), axis=1)
        d_out_all = lax.all_gather(d_out, "feat", axis=0, tiled=True)
        d_hidden = jnp.einsum(
            "hf,fn->hn", w_mix[layer], d_out_all, preferred_element_type=jnp.float32
        )
        sigma = jax.nn.sigmoid(pre)
        d_pre = d_hidden * sigma * (1.0 + pre * (1.0 - sigma))
        local_hbias = jnp.sum(d_pre, axis=1)
        d_round = d_pre.astype(jnp.bfloat16)
        local_node = jnp.einsum("fn,hn->fh", acts_keep, d_round, preferred_element_type=jnp.float32)
        local_msg = jnp.einsum(
            "fn,hn->fh", message_keep, d_round, preferred_element_type=jnp.float32
        )
        local_mix = jnp.einsum("hn,fn->hf", hidden, d_out_all, preferred_element_type=jnp.float32)
        sum_node, sum_msg, sum_mix, sum_hbias, sum_obias = lax.psum(
            (local_node, local_msg, local_mix, local_hbias, local_obias), "blk"
        )
        grads_node[layer] = sum_node + (
            w_node[layer].astype(jnp.float32) - anchor_node[layer].astype(jnp.float32)
        )
        grads_msg[layer] = sum_msg + (
            w_msg[layer].astype(jnp.float32) - anchor_msg[layer].astype(jnp.float32)
        )
        grads_mix[layer] = sum_mix + (
            w_mix[layer].astype(jnp.float32) - anchor_mix[layer].astype(jnp.float32)
        )
        grads_hbias[layer] = sum_hbias
        grads_obias[layer] = sum_obias
        if layer > 0:
            combined = jnp.concatenate([w_node[layer], w_msg[layer]], axis=0)
            both_terms = lax.psum_scatter(
                input_rows(
                    combined, d_round, feat_half, lax.axis_size("feat") * (2 * feat_half)
                ).astype(jnp.bfloat16),
                "feat",
                scatter_dimension=0,
                tiled=True,
            ).astype(jnp.float32)
            d_in = both_terms[:feat_half]
            d_message = both_terms[feat_half:]
            share = (d_message / degree[None, :]).astype(jnp.bfloat16)
            source = share.reshape(feat_half, block_rows, tile_size)
            empty = jnp.zeros((feat_half, window_blocks, tile_size), jnp.float32)
            parts = jnp.einsum(
                "fbi,bkij->fbkj", source, mask_values, preferred_element_type=jnp.float32
            )
            totals = empty.at[:, target.reshape(block_rows * slot_count)].add(
                parts.reshape(feat_half, block_rows * slot_count, tile_size)
            )
            pieces = jnp.moveaxis(totals.reshape(feat_half, 2 * reach_dev + 1, node_count), 1, 0)
            nothing = jnp.zeros((1, feat_half, node_count), jnp.float32)
            ahead = jnp.concatenate(
                [jnp.flip(pieces[reach_dev + 1 : 2 * reach_dev], 0), nothing], axis=0
            )
            behind = jnp.concatenate([pieces[1:reach_dev], nothing], axis=0)

            def move_up(carried, piece):
                return (
                    shifted(carried.astype(jnp.bfloat16), "blk", 1).astype(carried.dtype) + piece,
                    None,
                )

            def move_down(carried, piece):
                return (
                    shifted(carried.astype(jnp.bfloat16), "blk", -1).astype(carried.dtype) + piece,
                    None,
                )

            upper, unused_up = lax.scan(move_up, pieces[2 * reach_dev], ahead)
            lower, unused_down = lax.scan(move_down, pieces[0], behind)
            back = pieces[reach_dev] + upper + lower
            d_out = (d_out.astype(jnp.float32) + d_in + share.astype(jnp.float32) + back).astype(
                jnp.bfloat16
            )
    return (
        acts,
        jnp.stack(grads_node),
        jnp.stack(grads_msg),
        jnp.stack(grads_mix),
        jnp.stack(grads_hbias),
        jnp.stack(grads_obias),
    )


def solution(mesh):
    placed = (
        P(("member", "feat"), "blk"),
        P("member", None, "feat"),
        P("member", None, "feat"),
        P("member", "feat", None),
        P("member", "feat"),
        P("member", "feat"),
        P("member", None, "feat"),
        P("member", None, "feat"),
        P("member", "feat", None),
        P(("member", "feat"), "blk"),
        P(("member", "blk"), None),
        P(("member", "blk")),
        P(("member", "blk"), None, None, None),
    )
    return jax.shard_map(
        local,
        mesh=mesh,
        in_specs=placed,
        out_specs=(
            P(("member", "feat"), "blk"),
            P("member", None, "feat"),
            P("member", None, "feat"),
            P("member", "feat", None),
            P("member", "feat"),
            P("member", "feat"),
        ),
        check_vma=False,
    )
```

profile of v0, /device:TPU:0, one launch (start us, length us, event | category | flops | bytes accessed | tf_op | source)
XLA Modules:
  0.0 169.0 jit_solution(11927963865514137374)
XLA Ops:
  7.2 3.0 %collective-permute-start = (bf16[64,512]{1,0:T(8,128)(2,1)}, bf16[64,512]{1,0:T(8,128)(2,1)S(1)}, u32[]{:S(2)}, u32[]{:S(2)}) collective-permute-start(bf16[64,512]{1,0:T(8,128)(2,1)} %param.15), channel_id=1, source_target_pairs={{0,2},{2,4},{4,6},{6,8},{8,10},{10,12},{12,14},{14,0},{1,3},{3,5},... | collective-permute-start | bytes 196616 | tf_op jit(solution)/shard_map/while/body/eval_jaxpr/ppermute | solution.py:10
  10.2 3.1 %collective-permute-start.1 = (bf16[64,512]{1,0:T(8,128)(2,1)}, bf16[64,512]{1,0:T(8,128)(2,1)S(1)}, u32[]{:S(2)}, u32[]{:S(2)}) collective-permute-start(bf16[64,512]{1,0:T(8,128)(2,1)} %param.15), channel_id=1, source_target_pairs={{0,14},{2,0},{4,2},{6,4},{8,6},{10,8},{12,10},{14,12},{1,15},{3,1}... | collective-permute-start | bytes 196616 | tf_op jit(solution)/shard_map/while/body/eval_jaxpr/ppermute | solution.py:10
  13.3 2.1 %all_gather.18 = bf16[128,512]{1,0:T(8,128)(2,1)S(1)} all-gather(bf16[64,512]{1,0:T(8,128)(2,1)} %param.15), channel_id=1, replica_groups=mesh['member'=2,'blk'=8,'feat'=2] {'feat'}, dimensions={0}, use_global_device_ids=true | all-gather | bytes 196608 | tf_op jit(solution)/shard_map/all_gather | solution.py:85
  15.5 0.8 compare_and_fusion
  16.3 0.7 fusion.67
  17.1 2.6 %multiply_reduce_fusion = (s32[4,128]{1,0:T(4,128)S(1)}, bf16[4,12,128,128]{3,2,1,0:T(8,128)(2,1)S(1)}) fusion(s32[4,12,128,128]{3,2,1,0:T(8,128)} %param.27, s32[4,12]{1,0:T(4,128)S(1)} %fusion.67), kind=kLoop, calls=%fused_computation.4 | loop fusion | flops 2358784 | bytes 4720832 | tf_op jit(solution)/shard_map/reduce_sum | solution.py:59
  19.7 0.1 fusion.54
  20.1 0.9 gather_fusion
  20.9 1.9 %all_gather.22 = bf16[128,512]{1,0:T(8,128)(2,1)S(1)} all-gather(bf16[64,512]{1,0:T(8,128)(2,1)S(1)} %copy-done.12), channel_id=1, replica_groups=mesh['member'=2,'blk'=8,'feat'=2] {'feat'}, dimensions={0}, use_global_device_ids=true | all-gather | bytes 196608 | tf_op jit(solution)/shard_map/all_gather | solution.py:109
  22.9 0.2 copy.50
  23.1 0.2 reshape.202
  23.3 0.7 gather_fusion.1
  24.0 0.7 convolution_bitcast_fusion.3
  24.8 1.9 %all_gather.19 = bf16[128,512]{1,0:T(8,128)(2,1)S(1)} all-gather(bf16[64,512]{1,0:T(8,128)(2,1)S(1)} %fusion.16), channel_id=1, replica_groups=mesh['member'=2,'blk'=8,'feat'=2] {'feat'}, dimensions={0}, use_global_device_ids=true | all-gather | bytes 196608 | tf_op jit(solution)/shard_map/all_gather | solution.py:86
  26.7 0.2 multiply_convert_fusion.2
  26.9 0.2 convolution_bitcast_fusion.1
  27.1 0.8 copy.69
  28.1 6.4 %reduce-scatter.10.cloned.1.call-done = f32[64,512]{1,0:T(8,128)} async-done(((f32[128,512]{1,0:T(8,128)}), f32[64,512]{1,0:T(8,128)}) %reduce-scatter.10.cloned.1.call-update) | async-done | bytes 131088 | tf_op jit(solution)/shard_map/reduce_scatter | solution.py:94
  34.4 1.0 fusion.18
  35.4 1.8 %collective-permute-start.2 = (bf16[64,512]{1,0:T(8,128)(2,1)S(1)}, bf16[64,512]{1,0:T(8,128)(2,1)S(1)}, u32[]{:S(2)}, u32[]{:S(2)}) collective-permute-start(bf16[64,512]{1,0:T(8,128)(2,1)S(1)} %fusion.18), channel_id=1, source_target_pairs={{0,2},{2,4},{4,6},{6,8},{8,10},{10,12},{12,14},{14,0},{1,3},{3,5},... | collective-permute-start | bytes 196616 | tf_op jit(solution)/shard_map/while/body/eval_jaxpr/ppermute | solution.py:10
  37.2 3.0 %collective-permute-start.3 = (bf16[64,512]{1,0:T(8,128)(2,1)S(1)}, bf16[64,512]{1,0:T(8,128)(2,1)S(1)}, u32[]{:S(2)}, u32[]{:S(2)}) collective-permute-start(bf16[64,512]{1,0:T(8,128)(2,1)S(1)} %fusion.18), channel_id=1, source_target_pairs={{0,14},{2,0},{4,2},{6,4},{8,6},{10,8},{12,10},{14,12},{1,15},{3,1}... | collective-permute-start | bytes 196616 | tf_op jit(solution)/shard_map/while/body/eval_jaxpr/ppermute | solution.py:10
  40.2 1.9 %all_gather.20 = bf16[128,512]{1,0:T(8,128)(2,1)S(1)} all-gather(bf16[64,512]{1,0:T(8,128)(2,1)S(1)} %fusion.18), channel_id=1, replica_groups=mesh['member'=2,'blk'=8,'feat'=2] {'feat'}, dimensions={0}, use_global_device_ids=true | all-gather | bytes 196608 | tf_op jit(solution)/shard_map/all_gather | solution.py:85
  42.2 0.4 collective-permute-done.2
  42.6 0.2 collective-permute-done.3
  42.9 0.2 copy.54
  43.1 0.2 reshape.204
  43.3 0.7 gather_fusion.2
  44.0 0.7 convolution_bitcast_fusion.2
  44.8 1.9 %all_gather.21 = bf16[128,512]{1,0:T(8,128)(2,1)S(1)} all-gather(bf16[64,512]{1,0:T(8,128)(2,1)S(1)} %fusion.20), channel_id=1, replica_groups=mesh['member'=2,'blk'=8,'feat'=2] {'feat'}, dimensions={0}, use_global_device_ids=true | all-gather | bytes 196608 | tf_op jit(solution)/shard_map/all_gather | solution.py:86
  46.7 0.2 multiply_convert_fusion.1
  46.9 0.8 fusion.86
  47.6 1.0 convolution_convert_fusion
  48.7 0.8 fusion.74
  49.5 0.8 fusion.76
  50.2 0.9 convolution_bitcast_fusion
  51.1 6.6 %reduce-scatter.14.cloned.1.call-done = bf16[128,512]{1,0:T(8,128)(2,1)} async-done(((bf16[256,512]{1,0:T(8,128)(2,1)}), bf16[128,512]{1,0:T(8,128)(2,1)}) %reduce-scatter.14.cloned.1.call-update) | async-done | bytes 131088 | tf_op jit(solution)/shard_map/reduce_scatter | solution.py:138
  57.8 0.9 convert_element_type.161
  58.7 0.7 copy-done
  59.4 0.4 fusion.29
  59.8 2.9 %scatter_fusion = f32[64,12,128]{2,0,1:T(8,128)S(1)} fusion(f32[64,12,128]{2,0,1:T(8,128)S(1)} %broadcast_in_dim.61, s32[48]{0:T(128)S(1)} %fusion.73, f32[48,64,128]{2,1,0:T(8,128)S(1)} %bitcast.188), kind=kCustom, calls=%fused_computation.3 | custom fusion | flops 393216 | bytes 4718784 | tf_op jit(solution)/shard_map/scatter-add | solution.py:154
  62.8 0.2 copy.62
  63.1 0.2 reshape.209
  63.4 1.8 %collective-permute-start.4 = (bf16[64,512]{1,0:T(8,128)(2,1)S(1)}, bf16[64,512]{1,0:T(8,128)(2,1)S(1)}, u32[]{:S(2)}, u32[]{:S(2)}) collective-permute-start(bf16[64,512]{1,0:T(8,128)(2,1)S(1)} %get-tuple-element.79), channel_id=1, source_target_pairs={{0,2},{2,4},{4,6},{6,8},{8,10},{10,12},{12,14},{14,0},{1,3},{3,5},... | collective-permute-start | bytes 196616 | tf_op jit(solution)/shard_map/while/body/eval_jaxpr/ppermute | solution.py:10
  65.2 3.0 %collective-permute-start.5 = (bf16[64,512]{1,0:T(8,128)(2,1)S(1)}, bf16[64,512]{1,0:T(8,128)(2,1)S(1)}, u32[]{:S(2)}, u32[]{:S(2)}) collective-permute-start(bf16[64,512]{1,0:T(8,128)(2,1)S(1)} %get-tuple-element.80), channel_id=1, source_target_pairs={{0,14},{2,0},{4,2},{6,4},{8,6},{10,8},{12,10},{14,12},{1,15},{3,1}... | collective-permute-start | bytes 196616 | tf_op jit(solution)/shard_map/while/body/eval_jaxpr/ppermute | solution.py:10
  68.2 0.8 fusion.89
  69.0 0.8 copy.71
  69.9 0.7 collective-permute-done.4
  70.6 0.2 collective-permute-done.5
  70.9 0.7 convert_reduce_fusion.1
  71.6 2.0 %all_gather.23 = bf16[128,512]{1,0:T(8,128)(2,1)S(1)} all-gather(bf16[64,512]{1,0:T(8,128)(2,1)S(1)} %get-tuple-element.72), channel_id=1, replica_groups=mesh['member'=2,'blk'=8,'feat'=2] {'feat'}, dimensions={0}, use_global_device_ids=true | all-gather | bytes 196608 | tf_op jit(solution)/shard_map/all_gather | solution.py:109
  73.6 0.8 fusion.87
  74.5 0.8 fusion.88
  75.2 0.8 fusion.45
  76.0 0.8 convolution_bitcast_fusion.6
  76.9 1.6 fusion.22
  78.5 77.3 %all-reduce.3.cloned.1.call-done = (f32[128,64]{0,1:T(8,128)}, f32[128,64]{0,1:T(8,128)}, f32[128,64]{0,1:T(8,128)}, f32[128,64]{0,1:T(8,128)}, f32[64,128]{1,0:...) async-done(((f32[128,64]{0,1:T(8,128)}, f32[128,64]{0,1:T(8,128)}, f32[128,64]{0,1:T(8,128)}, ...) | async-done | bytes 197648 | tf_op jit(solution)/shard_map/psum | solution.py:122
  155.8 1.2 pad_maximum_fusion.5
  157.0 1.2 pad_maximum_fusion.4
  158.2 0.8 fusion.36
  159.0 0.6 pad_maximum_fusion.2
  159.7 0.8 fusion.40
  160.4 0.6 pad_maximum_fusion.1
  161.1 0.8 fusion.44
  161.9 0.6 pad_maximum_fusion
  (90 shorter events, 1.3 us)
Async XLA Ops:
  7.2 27.3 %reduce-scatter.10.cloned.1.call-start = ((), (), s32[]{:S(2)}) async-start(), calls=%async_computation.3 | async-start | bytes 393216 | tf_op jit(solution)/shard_map/reduce_scatter | solution.py:94
  7.2 15.6 %collective-permute-start = (bf16[64,512]{1,0:T(8,128)(2,1)}, bf16[64,512]{1,0:T(8,128)(2,1)S(1)}, u32[]{:S(2)}, u32[]{:S(2)}) collective-permute-start(bf16[64,512]{1,0:T(8,128)(2,1)} %param.15), channel_id=1, source_target_pairs={{0,2},{2,4},{4,6},{6,8},{8,10},{10,12},{12,14},{14,0},{1,3},{3,5},... | collective-permute-start | bytes 196616 | tf_op jit(solution)/shard_map/while/body/eval_jaxpr/ppermute | solution.py:10
  10.2 12.6 %collective-permute-start.1 = (bf16[64,512]{1,0:T(8,128)(2,1)}, bf16[64,512]{1,0:T(8,128)(2,1)S(1)}, u32[]{:S(2)}, u32[]{:S(2)}) collective-permute-start(bf16[64,512]{1,0:T(8,128)(2,1)} %param.15), channel_id=1, source_target_pairs={{0,14},{2,0},{4,2},{6,4},{8,6},{10,8},{12,10},{14,12},{1,15},{3,1}... | collective-permute-start | bytes 196616 | tf_op jit(solution)/shard_map/while/body/eval_jaxpr/ppermute | solution.py:10
  15.4 4.2 %copy-start.4 = (bf16[128,512]{1,0:T(8,128)(2,1)}, bf16[128,512]{1,0:T(8,128)(2,1)S(1)}, u32[]{:S(2)}) copy-start(bf16[128,512]{1,0:T(8,128)(2,1)S(1)} %all_gather.18) | copy-start | bytes 393220
  17.0 2.6 %copy-start.25 = (f32[2,64]{1,0:T(2,128)S(1)}, f32[2,64]{1,0:T(2,128)}, u32[]{:S(2)}) copy-start(f32[2,64]{1,0:T(2,128)} %param.19) | copy-start | bytes 1540
  17.0 2.6 %copy-start.18 = (bf16[2,128,64]{1,2,0:T(8,128)(2,1)S(1)}, bf16[2,128,64]{1,2,0:T(8,128)(2,1)}, u32[]{:S(2)}) copy-start(bf16[2,128,64]{1,2,0:T(8,128)(2,1)} %param.16) | copy-start | bytes 98308
  17.0 2.8 %copy-start.21 = (bf16[2,128,64]{1,2,0:T(8,128)(2,1)S(1)}, bf16[2,128,64]{1,2,0:T(8,128)(2,1)}, u32[]{:S(2)}) copy-start(bf16[2,128,64]{1,2,0:T(8,128)(2,1)} %param.17) | copy-start | bytes 98308
  17.0 3.9 %copy-start.12 = (bf16[64,512]{1,0:T(8,128)(2,1)S(1)}, bf16[64,512]{1,0:T(8,128)(2,1)}, u32[]{:S(2)}) copy-start(bf16[64,512]{1,0:T(8,128)(2,1)} %param.24) | copy-start | bytes 196612
  17.1 5.8 %copy-start.7 = (bf16[64,512]{1,0:T(8,128)(2,1)S(1)}, bf16[64,512]{1,0:T(8,128)(2,1)}, u32[]{:S(2)}) copy-start(bf16[64,512]{1,0:T(8,128)(2,1)} %param.15) | copy-start | bytes 196612
  22.8 24.0 %copy-start.10 = (bf16[128,512]{1,0:T(8,128)(2,1)}, bf16[128,512]{1,0:T(8,128)(2,1)S(1)}, u32[]{:S(2)}) copy-start(bf16[128,512]{1,0:T(8,128)(2,1)S(1)} %all_gather.22) | copy-start | bytes 393220
  24.0 2.9 %copy-start.20 = (bf16[2,64,128]{2,1,0:T(8,128)(2,1)S(1)}, bf16[2,64,128]{2,1,0:T(8,128)(2,1)}, u32[]{:S(2)}) copy-start(bf16[2,64,128]{2,1,0:T(8,128)(2,1)} %param.18) | copy-start | bytes 98308
  24.7 3.3 %copy-start.26 = (f32[2,64]{1,0:T(2,128)S(1)}, f32[2,64]{1,0:T(2,128)}, u32[]{:S(2)}) copy-start(f32[2,64]{1,0:T(2,128)} %param.20) | copy-start | bytes 1540
  26.7 10.5 %copy-start.8 = (bf16[128,512]{1,0:T(8,128)(2,1)}, bf16[128,512]{1,0:T(8,128)(2,1)S(1)}, u32[]{:S(2)}) copy-start(bf16[128,512]{1,0:T(8,128)(2,1)S(1)} %all_gather.19) | copy-start | bytes 393220
  26.9 16.4 %copy-start.14 = (bf16[64,512]{1,0:T(8,128)(2,1)}, bf16[64,512]{1,0:T(8,128)(2,1)S(1)}, u32[]{:S(2)}) copy-start(bf16[64,512]{1,0:T(8,128)(2,1)S(1)} %get-tuple-element.92) | copy-start | bytes 196612
  28.0 29.8 %reduce-scatter.14.cloned.1.call-start = ((), (), s32[]{:S(2)}) async-start(), calls=%async_computation.5 | async-start | bytes 393216 | tf_op jit(solution)/shard_map/reduce_scatter | solution.py:138
  35.4 9.3 %copy-start.2 = (bf16[64,512]{1,0:T(8,128)(2,1)}, bf16[64,512]{1,0:T(8,128)(2,1)S(1)}, u32[]{:S(2)}) copy-start(bf16[64,512]{1,0:T(8,128)(2,1)S(1)} %fusion.18) | copy-start | bytes 196612
  35.4 7.2 %collective-permute-start.2 = (bf16[64,512]{1,0:T(8,128)(2,1)S(1)}, bf16[64,512]{1,0:T(8,128)(2,1)S(1)}, u32[]{:S(2)}, u32[]{:S(2)}) collective-permute-start(bf16[64,512]{1,0:T(8,128)(2,1)S(1)} %fusion.18), channel_id=1, source_target_pairs={{0,2},{2,4},{4,6},{6,8},{8,10},{10,12},{12,14},{14,0},{1,3},{3,5},... | collective-permute-start | bytes 196616 | tf_op jit(solution)/shard_map/while/body/eval_jaxpr/ppermute | solution.py:10
  37.2 5.7 %collective-permute-start.3 = (bf16[64,512]{1,0:T(8,128)(2,1)S(1)}, bf16[64,512]{1,0:T(8,128)(2,1)S(1)}, u32[]{:S(2)}, u32[]{:S(2)}) collective-permute-start(bf16[64,512]{1,0:T(8,128)(2,1)S(1)} %fusion.18), channel_id=1, source_target_pairs={{0,14},{2,0},{4,2},{6,4},{8,6},{10,8},{12,10},{14,12},{1,15},{3,1}... | collective-permute-start | bytes 196616 | tf_op jit(solution)/shard_map/while/body/eval_jaxpr/ppermute | solution.py:10
  46.8 12.6 %copy-start.16 = (bf16[64,512]{1,0:T(8,128)(2,1)}, bf16[64,512]{1,0:T(8,128)(2,1)S(1)}, u32[]{:S(2)}) copy-start(bf16[64,512]{1,0:T(8,128)(2,1)S(1)} %get-tuple-element.94) | copy-start | bytes 196612
  48.6 28.2 %reduce-scatter.12.cloned.1.call-start = ((), (), s32[]{:S(2)}) async-start(), calls=%async_computation.4 | async-start | bytes 393216 | tf_op jit(solution)/shard_map/reduce_scatter | solution.py:94
  58.7 0.7 copy-start
  62.8 5.4 %copy-start.11 = (bf16[128,512]{1,0:T(8,128)(2,1)S(1)}, bf16[128,512]{1,0:T(8,128)(2,1)}, u32[]{:S(2)}) copy-start(bf16[128,512]{1,0:T(8,128)(2,1)} %copy-done.10) | copy-start | bytes 393220
  62.8 5.4 %copy-start.17 = (bf16[64,512]{1,0:T(8,128)(2,1)S(1)}, bf16[64,512]{1,0:T(8,128)(2,1)}, u32[]{:S(2)}) copy-start(bf16[64,512]{1,0:T(8,128)(2,1)} %copy-done.16) | copy-start | bytes 196612
  62.8 6.2 %copy-start.6 = (f32[128,512]{0,1:T(8,128)S(1)}, f32[128,512]{0,1:T(8,128)}, u32[]{:S(2)}) copy-start(f32[128,512]{0,1:T(8,128)} %convolution_bitcast_fusion) | copy-start | bytes 786436
  63.1 7.8 %copy-start.1 = (f32[128,512]{1,0:T(8,128)S(1)}, f32[128,512]{1,0:T(8,128)}, u32[]{:S(2)}) copy-start(f32[128,512]{1,0:T(8,128)} %copy-done) | copy-start | bytes 786436
  63.1 7.8 %copy-start.13 = (bf16[64,512]{1,0:T(8,128)(2,1)S(1)}, bf16[64,512]{1,0:T(8,128)(2,1)}, u32[]{:S(2)}) copy-start(bf16[64,512]{1,0:T(8,128)(2,1)} %param.24) | copy-start | bytes 196612
  63.4 11.1 %copy-start.15 = (bf16[64,512]{1,0:T(8,128)(2,1)S(1)}, bf16[64,512]{1,0:T(8,128)(2,1)}, u32[]{:S(2)}) copy-start(bf16[64,512]{1,0:T(8,128)(2,1)} %copy-done.14) | copy-start | bytes 196612
  63.4 11.8 %copy-start.9 = (bf16[128,512]{1,0:T(8,128)(2,1)S(1)}, bf16[128,512]{1,0:T(8,128)(2,1)}, u32[]{:S(2)}) copy-start(bf16[128,512]{1,0:T(8,128)(2,1)} %copy-done.8) | copy-start | bytes 393220
  63.4 7.2 %collective-permute-start.4 = (bf16[64,512]{1,0:T(8,128)(2,1)S(1)}, bf16[64,512]{1,0:T(8,128)(2,1)S(1)}, u32[]{:S(2)}, u32[]{:S(2)}) collective-permute-start(bf16[64,512]{1,0:T(8,128)(2,1)S(1)} %get-tuple-element.79), channel_id=1, source_target_pairs={{0,2},{2,4},{4,6},{6,8},{8,10},{10,12},{12,14},{14,0},{1,3},{3,5},... | collective-permute-start | bytes 196616 | tf_op jit(solution)/shard_map/while/body/eval_jaxpr/ppermute | solution.py:10
  65.2 10.8 %copy-start.5 = (bf16[128,512]{1,0:T(8,128)(2,1)S(1)}, bf16[128,512]{1,0:T(8,128)(2,1)}, u32[]{:S(2)}) copy-start(bf16[128,512]{1,0:T(8,128)(2,1)} %copy-done.4) | copy-start | bytes 393220
  65.2 5.7 %collective-permute-start.5 = (bf16[64,512]{1,0:T(8,128)(2,1)S(1)}, bf16[64,512]{1,0:T(8,128)(2,1)S(1)}, u32[]{:S(2)}, u32[]{:S(2)}) collective-permute-start(bf16[64,512]{1,0:T(8,128)(2,1)S(1)} %get-tuple-element.80), channel_id=1, source_target_pairs={{0,14},{2,0},{4,2},{6,4},{8,6},{10,8},{12,10},{14,12},{1,15},{3,1}... | collective-permute-start | bytes 196616 | tf_op jit(solution)/shard_map/while/body/eval_jaxpr/ppermute | solution.py:10
  69.0 7.9 %copy-start.3 = (bf16[64,512]{1,0:T(8,128)(2,1)S(1)}, bf16[64,512]{1,0:T(8,128)(2,1)}, u32[]{:S(2)}) copy-start(bf16[64,512]{1,0:T(8,128)(2,1)} %copy-done.2) | copy-start | bytes 196612
  69.8 88.4 %copy-start.22 = (bf16[2,64,128]{2,1,0:T(8,128)(2,1)S(1)}, bf16[2,64,128]{2,1,0:T(8,128)(2,1)}, u32[]{:S(2)}) copy-start(bf16[2,64,128]{2,1,0:T(8,128)(2,1)} %param.23) | copy-start | bytes 98308
  69.8 86.0 %all-reduce.3.cloned.1.call-start = ((), (), s32[]{:S(2)}) async-start(), calls=%async_computation.6 | async-start | bytes 397312 | tf_op jit(solution)/shard_map/psum | solution.py:122
  70.9 88.8 %copy-start.23 = (bf16[2,128,64]{1,2,0:T(8,128)(2,1)S(1)}, bf16[2,128,64]{1,2,0:T(8,128)(2,1)}, u32[]{:S(2)}) copy-start(bf16[2,128,64]{1,2,0:T(8,128)(2,1)} %param.22) | copy-start | bytes 98308
  71.6 89.5 %copy-start.19 = (bf16[2,128,64]{1,2,0:T(8,128)(2,1)S(1)}, bf16[2,128,64]{1,2,0:T(8,128)(2,1)}, u32[]{:S(2)}) copy-start(bf16[2,128,64]{1,2,0:T(8,128)(2,1)} %param.16) | copy-start | bytes 98308
  71.6 89.5 %copy-start.24 = (bf16[2,128,64]{1,2,0:T(8,128)(2,1)S(1)}, bf16[2,128,64]{1,2,0:T(8,128)(2,1)}, u32[]{:S(2)}) copy-start(bf16[2,128,64]{1,2,0:T(8,128)(2,1)} %param.21) | copy-start | bytes 98308
Sparse Core Ops, SparseCore 0:
  28.1 6.2 reduce-scatter.9
  48.8 8.9 reduce-scatter.13
  70.0 6.2 reduce-scatter.11
  82.0 73.7 all-reduce.2
where the time goes:
time: 170 us; the launch traced here: 169 us
  waiting for transfers between devices  92 us (54%)
  other arithmetic  18.2 us (11%)
  starting transfers between devices  15.8 us (9%)
  between operations  14.3 us (8%)
  blocking collectives  11.7 us (7%)
  matrix products  10.7 us (6%)
  local copies, waits for them, and re-layouts  6.29 us (4%)
    psum x1, waiting for transfers between devices, local(): lax.psum((local_node, local_msg, local_mix, local_hbias, local_obias), 'b...  77.3 us
    ppermute x6, starting transfers between devices, shifted(): return lax.ppermute(value, axis, pairs)  15.7 us
    reduce_scatter x1, waiting for transfers between devices, local(): lax.psum_scatter(input_rows(combined, d_round, feat_half, lax.axis_size('...  6.62 us
    reduce_scatter x2, waiting for transfers between devices, local(): lax.psum_scatter(mix_rows(w_mix[layer], hidden), 'feat', scatter_dimensio...  6.38 us
    all_gather x2, blocking collectives, local(): lax.all_gather(acts, 'feat', axis=0, tiled=True)  3.99 us
    all_gather x2, blocking collectives, local(): d_out_all = lax.all_gather(d_out, 'feat', axis=0, tiled=True)  3.92 us
    all_gather x2, blocking collectives, local(): lax.all_gather(message, 'feat', axis=0, tiled=True)  3.8 us
  transfers between devices with their start and end apart: 10, of which 7 were waited for; matrix products, arithmetic and copies ran while one was open for 9% of the time, Pallas kernels for 0%

commit v1 on v0

v1 whole, which is shorter than its diff:
```python
import functools

import jax
import jax.numpy as jnp
from jax import lax
from jax.experimental import pallas as pl
from jax.experimental.pallas import tpu as pltpu
from jax.sharding import PartitionSpec as P

F32 = jnp.float32
BF16 = jnp.bfloat16
MESH = pl.DeviceIdType.MESH


def mm(left, right):
    return jnp.dot(left, right, preferred_element_type=F32)


def mm_nt(left, right):
    return lax.dot_general(left, right, (((1,), (1,)), ((), ())), preferred_element_type=F32)


def eye(size):
    rows = lax.broadcasted_iota(jnp.int32, (size, size), 0)
    cols = lax.broadcasted_iota(jnp.int32, (size, size), 1)
    return rows == cols


def to_column(row):
    size = row.shape[1]
    return jnp.sum(jnp.where(eye(size), jnp.broadcast_to(row, (size, size)), 0.0), axis=1, keepdims=True)


def to_row(column):
    size = column.shape[0]
    return jnp.sum(jnp.where(eye(size), jnp.broadcast_to(column, (size, size)), 0.0), axis=0, keepdims=True)


def kernel(
    n, reach, layers, br, slots, tile, half, nodes,
    cols, count, feats, w_node, w_msg, w_mix, hbias, obias, a_node, a_msg, a_mix, cot, masks,
    out_x, g_node, g_msg, g_mix, g_hb, g_ob,
    mask_v, mask_b, adj, xwin, xm, wt, wmix, wmixt, wback, bias, dy, pre_s, hid, dr, dh, part_out, part_in,
    gbuf, grecv, gred,
    s_mask, s_xs, s_xr, s_ps, s_pr, s_fs, s_fr, s_gs, s_gr, s_as, s_ar,
):
    feat = 2 * half
    me = lax.axis_index("blk")
    side = lax.axis_index("feat")
    peer = 1 - side
    wins = 2 * reach + 1
    own = pl.ds(pl.multiple_of(side * half, half), half)
    own_msg = pl.ds(pl.multiple_of(feat + side * half, half), half)
    far = pl.ds(pl.multiple_of(peer * half, half), half)
    chunk = gbuf.shape[2]

    def at(step):
        return lax.rem(me + step + n, n)

    barrier = pltpu.get_barrier_semaphore()
    pl.semaphore_signal(barrier, inc=1, device_id={"feat": peer}, device_id_type=MESH)
    for step in range(1, n):
        pl.semaphore_signal(barrier, inc=1, device_id={"blk": at(step)}, device_id_type=MESH)

    mask_copies = [pltpu.make_async_copy(masks.at[r], mask_v.at[r], s_mask.at[r]) for r in range(br)]
    for copy in mask_copies:
        copy.start()

    xm[0, own] = feats[...]
    xwin[0, reach] = feats[...]
    dy[layers - 1, own] = cot[...]
    unit = jnp.where(eye(half), 1.0, 0.0).astype(BF16)
    for l in range(layers):
        wt[l, own, 0:feat] = mm_nt(unit, w_node[l]).astype(BF16)
        wt[l, own, feat : 2 * feat] = mm_nt(unit, w_msg[l]).astype(BF16)
        wmix[l, own] = w_mix[l]
    bias[side] = jnp.zeros(bias.shape[1:], F32)
    bias[side, 0:layers, 0:half] = hbias[...]
    bias[side, layers : 2 * layers, 0:half] = obias[...]

    pl.semaphore_wait(barrier, n)

    pending = []

    def send(src, dst, s_send, s_recv, device):
        copy = pltpu.make_async_remote_copy(
            src_ref=src, dst_ref=dst, send_sem=s_send, recv_sem=s_recv, device_id=device, device_id_type=MESH
        )
        copy.start()
        pending.append(copy)
        return copy

    def spread_out(src, l):
        copies = []
        for step in range(1, reach + 1):
            for sign in (1, -1):
                slot = reach - sign * step
                copies.append(
                    (slot, send(src, xwin.at[l, slot], s_xs.at[l, slot], s_xr.at[l, slot], {"blk": at(sign * step)}))
                )
        return copies

    def to_peer(index, src, dst):
        return send(src, dst, s_fs.at[index], s_fr.at[index], {"feat": peer})

    arriving = spread_out(feats, 0)
    first = [
        to_peer(0, wmix.at[:, own], wmix.at[:, own]),
        to_peer(1, wt.at[:, own], wt.at[:, own]),
        to_peer(2, bias.at[side], bias.at[side]),
        to_peer(3, dy.at[layers - 1, own], dy.at[layers - 1, own]),
        to_peer(4, xm.at[0, own], xm.at[0, own]),
    ]

    for r in range(br):
        mask_copies[r].wait()

    def build_row(r, unused):
        for k in range(slots):
            mask_b[k] = mask_v[r, k].astype(F32).astype(BF16)
        live = count[r]
        targets = []
        for k in range(slots):
            name = cols[r, k]
            block = lax.rem(lax.div(name, br) - me + reach + n, n) * br + lax.rem(name, br)
            targets.append(jnp.where(k < live, block, -1))

        def build_dev(j, unused):
            rows = pl.ds(pl.multiple_of(r * tile, tile), tile)
            for c in range(br):
                total = jnp.zeros((tile, tile), BF16)
                for k in range(slots):
                    hit = jnp.where(targets[k] == j * br + c, 1.0, 0.0).astype(F32)
                    total = total + jnp.full((tile, tile), hit, F32).astype(BF16) * mask_b[k]
                adj[j, rows, c * tile : (c + 1) * tile] = total
            return unused

        return lax.fori_loop(0, wins, build_dev, unused)

    lax.fori_loop(0, br, build_row, 0)
    ones = jnp.ones((16, nodes), BF16)
    degree = mm_nt(ones, adj[0])
    for j in range(1, wins):
        degree = degree + mm_nt(ones, adj[j])
    inverse = 1.0 / (degree[0:1] + 1.0)

    for copy in first[0:4]:
        copy.wait_recv()
    unit_f = jnp.where(eye(feat), 1.0, 0.0).astype(BF16)
    hb, ob = [], []
    for l in range(layers):
        wmixt[l] = mm_nt(unit_f, wmix[l]).astype(BF16)
        if l > 0:
            wback[l, 0:feat] = mm_nt(unit_f, wt[l, :, 0:feat]).astype(BF16)
            wback[l, feat : 2 * feat] = mm_nt(unit_f, wt[l, :, feat : 2 * feat]).astype(BF16)
        hb.append(
            jnp.concatenate([to_column(bias[s, l : l + 1, 0:half]) for s in range(2)], axis=0)
        )
        ob.append([to_column(bias[s, layers + l : layers + l + 1, 0:half]) for s in (side, peer)])
    dh[...] = mm(wmix[layers - 1], dy[layers - 1])
    first[4].wait_recv()

    for l in range(layers):
        summed = mm_nt(xwin[l, reach], adj[reach])
        for slot, copy in arriving:
            copy.wait_recv()
            summed = summed + mm_nt(xwin[l, slot], adj[slot])
        message = (xm[l, own].astype(F32) + summed) * inverse
        xm[l, own_msg] = message.astype(BF16)
        copy = to_peer(5 + l, xm.at[l, own_msg], xm.at[l, own_msg])
        part = mm(wt[l, :, 0:feat], xm[l, 0:feat]) + hb[l]
        copy.wait_recv()
        pre = part + mm(wt[l, :, feat : 2 * feat], xm[l, feat : 2 * feat])
        sigma = 1.0 / (1.0 + jnp.exp(-pre))
        hidden = (pre * sigma).astype(BF16)
        hid[l] = hidden
        slope = sigma * (1.0 + pre * (1.0 - sigma))
        pre_s[l] = slope
        if l + 1 < layers:
            after = (xm[l, own].astype(F32) + mm(wmixt[l, own], hidden) + ob[l][0]).astype(BF16)
            xm[l + 1, own] = after
            xwin[l + 1, reach] = after
            arriving = spread_out(xwin.at[l + 1, reach], l + 1)
            xm[l + 1, far] = (xm[l, far].astype(F32) + mm(wmixt[l, far], hidden) + ob[l][1]).astype(BF16)

    def reduce_start(l):
        copies = []
        for step in range(1, n):
            to = at(step)
            copies.append(
                send(gbuf.at[l, to], grecv.at[l, step - 1], s_gs.at[l, step - 1], s_gr.at[l, step - 1], {"blk": to})
            )
        return copies

    def reduce_end(l, copies):
        total = gbuf[l, me]
        for step in range(1, n):
            copies[step - 1].wait_recv()
            total = total + grecv[l, step - 1]
        gred[l, me] = total
        return [
            send(gred.at[l, me], gred.at[l, me], s_as.at[l, step - 1], s_ar.at[l, step - 1], {"blk": at(step)})
            for step in range(1, n)
        ]

    def finish(l, copies):
        for copy in copies:
            copy.wait_recv()
        per = feat // chunk
        both = gred[l, 0:per].reshape(feat, 2 * half)
        g_node[l] = both[:, 0:half] + (w_node[l].astype(F32) - a_node[l].astype(F32))
        g_msg[l] = both[:, half : 2 * half] + (w_msg[l].astype(F32) - a_msg[l].astype(F32))
        more = half // chunk
        mixed = gred[l, per : per + more].reshape(half, feat)
        g_mix[l] = mixed + (w_mix[l].astype(F32) - a_mix[l].astype(F32))
        g_hb[l : l + 1] = gred[l, per + more, 0:1, 0:half]
        g_ob[l : l + 1] = gred[l, per + more, 1:2, 0:half]

    def gradients(l, d_own, d_round_own, dy_own):
        zero = jnp.zeros((half, nodes), BF16)
        both = mm_nt(xm[l, 0:feat], jnp.concatenate([d_round_own, zero], axis=0)) + mm_nt(
            xm[l, feat : 2 * feat], jnp.concatenate([zero, d_round_own], axis=0)
        )
        per = feat // chunk
        more = half // chunk
        gbuf[l, 0:per] = both.reshape(per, chunk, 2 * half)
        gbuf[l, per : per + more] = mm_nt(hid[l, own], dy[l]).reshape(more, chunk, feat)
        gbuf[l, per + more :] = jnp.zeros((n - per - more, chunk, 2 * half), F32)
        gbuf[l, per + more, 0:1, 0:half] = to_row(jnp.sum(d_own, axis=1, keepdims=True))
        gbuf[l, per + more, 1:2, 0:half] = to_row(jnp.sum(dy_own, axis=1, keepdims=True))

    reducing = {}
    for l in range(layers - 1, -1, -1):
        dy_own = dy[l, own].astype(F32)
        if l > 0:
            if l < layers - 1:
                dh[...] = mm(wmix[l], dy[l])
            d_pre = dh[...] * pre_s[l]
            d_round = d_pre.astype(BF16)
            dr[...] = d_round
            dh[...] = d_pre
            share = (mm(wback[l, own_msg], d_round) * inverse).astype(BF16)
            incoming = []
            for step in range(1, reach + 1):
                for sign in (1, -1):
                    slot = reach + sign * step
                    part_out[l - 1, slot] = mm(share, adj[slot]).astype(BF16)
                    landing = reach - sign * step
                    incoming.append(
                        (
                            landing,
                            send(
                                part_out.at[l - 1, slot],
                                part_in.at[l - 1, landing],
                                s_ps.at[l - 1, landing],
                                s_pr.at[l - 1, landing],
                                {"blk": at(sign * step)},
                            ),
                        )
                    )
            before = dy_own + mm(wback[l, own], d_round) + share.astype(F32) + mm(share, adj[reach])
            if l == layers - 1:
                last = xm[l, own].astype(F32) + mm(wmixt[l, own], hid[l]) + ob[l][0]
                out_x[...] = last.astype(BF16)
            gradients(l, dh[own], dr[own], dy_own)
            reducing[l] = reduce_start(l)
            for landing, copy in incoming:
                copy.wait_recv()
                before = before + part_in[l - 1, landing].astype(F32)
            dy[l - 1, own] = before.astype(BF16)
            copy = to_peer(5 + layers + l, dy.at[l - 1, own], dy.at[l - 1, own])
            copy.wait_recv()
        else:
            d_own = mm(wmix[l, own], dy[l]) * pre_s[l, own]
            gradients(l, d_own, d_own.astype(BF16), dy_own)
            reducing[l] = reduce_start(l)
    sharing = {}
    for l in range(layers - 1, -1, -1):
        sharing[l] = reduce_end(l, reducing[l])
    for l in range(layers - 1, -1, -1):
        finish(l, sharing[l])
    for copy in pending:
        copy.wait_send()


def local(
    features, w_node, w_msg, w_mix, hbias, obias, anchor_node, anchor_msg, anchor_mix, cotangent,
    tile_cols, tile_count, tile_masks,
):
    br, slots, tile, _ = tile_masks.shape
    half, nodes = features.shape
    feat = 2 * half
    layers = w_node.shape[0]
    n = lax.axis_size("blk")
    reach = max(1, n // 8)
    wins = 2 * reach + 1
    chunk = max(8, 256 // n)
    dma = pltpu.SemaphoreType.DMA
    vmem = pl.BlockSpec(memory_space=pltpu.VMEM)
    smem = pl.BlockSpec(memory_space=pltpu.SMEM)
    return pl.pallas_call(
        functools.partial(kernel, n, reach, layers, br, slots, tile, half, nodes),
        out_shape=(
            jax.ShapeDtypeStruct((half, nodes), BF16),
            jax.ShapeDtypeStruct((layers, feat, half), F32),
            jax.ShapeDtypeStruct((layers, feat, half), F32),
            jax.ShapeDtypeStruct((layers, half, feat), F32),
            jax.ShapeDtypeStruct((layers, half), F32),
            jax.ShapeDtypeStruct((layers, half), F32),
        ),
        in_specs=[smem, smem] + [vmem] * 10 + [pl.BlockSpec(memory_space=pl.ANY)],
        out_specs=(vmem,) * 6,
        scratch_shapes=[
            pltpu.VMEM((br, slots, tile, tile), jnp.int32),
            pltpu.VMEM((slots, tile, tile), BF16),
            pltpu.VMEM((wins, nodes, nodes), BF16),
            pltpu.VMEM((layers, wins, half, nodes), BF16),
            pltpu.VMEM((layers, 2 * feat, nodes), BF16),
            pltpu.VMEM((layers, feat, 2 * feat), BF16),
            pltpu.VMEM((layers, feat, feat), BF16),
            pltpu.VMEM((layers, feat, feat), BF16),
            pltpu.VMEM((layers, 2 * feat, feat), BF16),
            pltpu.VMEM((2, 8, 128), F32),
            pltpu.VMEM((layers, feat, nodes), BF16),
            pltpu.VMEM((layers, feat, nodes), F32),
            pltpu.VMEM((layers, feat, nodes), BF16),
            pltpu.VMEM((feat, nodes), BF16),
            pltpu.VMEM((feat, nodes), F32),
            pltpu.VMEM((layers - 1, wins, half, nodes), BF16),
            pltpu.VMEM((layers - 1, wins, half, nodes), BF16),
            pltpu.VMEM((layers, n, chunk, feat), F32),
            pltpu.VMEM((layers, n - 1, chunk, feat), F32),
            pltpu.VMEM((layers, n, chunk, feat), F32),
            dma((br,)),
            dma((layers, wins)),
            dma((layers, wins)),
            dma((layers - 1, wins)),
            dma((layers - 1, wins)),
            dma((5 + 2 * layers + 1,)),
            dma((5 + 2 * layers + 1,)),
            dma((layers, n - 1)),
            dma((layers, n - 1)),
            dma((layers, n - 1)),
            dma((layers, n - 1)),
        ],
        compiler_params=pltpu.CompilerParams(
            collective_id=0, has_side_effects=True, vmem_limit_bytes=50 * 1024 * 1024
        ),
        name="graph_net",
    )(
        tile_cols, tile_count, features, w_node, w_msg, w_mix, hbias, obias,
        anchor_node, anchor_msg, anchor_mix, cotangent, tile_masks,
    )


def solution(mesh):
    placed = (
        P(("member", "feat"), "blk"),
        P("member", None, "feat"),
        P("member", None, "feat"),
        P("member", "feat", None),
        P("member", "feat"),
        P("member", "feat"),
        P("member", None, "feat"),
        P("member", None, "feat"),
        P("member", "feat", None),
        P(("member", "feat"), "blk"),
        P(("member", "blk"), None),
        P(("member", "blk")),
        P(("member", "blk"), None, None, None),
    )
    return jax.shard_map(
        local,
        mesh=mesh,
        in_specs=placed,
        out_specs=(
            P(("member", "feat"), "blk"),
            P("member", None, "feat"),
            P("member", None, "feat"),
            P("member", "feat", None),
            P("member", "feat"),
            P("member", "feat"),
        ),
        check_vma=False,
    )
```

time: 170 us -> 53.8 us (0.32)
  waiting for transfers between devices: 92 us -> 0 us
  Pallas kernels: 0 us -> 37.3 us
  other arithmetic: 18.2 us -> 0 us
  starting transfers between devices: 15.8 us -> 0 us
  between operations: 14.3 us -> 0.67 us
  blocking collectives: 11.7 us -> 0 us
  matrix products: 10.7 us -> 0 us
  local copies, waits for them, and re-layouts: 6.29 us -> 15.1 us
    psum x1 -> x0, waiting for transfers between devices: 77.3 us -> none  [local(): lax.psum((local_node, local_msg, local_mix, local_hbias, local_obias), 'b...]
    pallas_call x0 -> x1, Pallas kernels: none -> 37.3 us  [local(): pl.pallas_call(functools.partial(kernel, n, reach, layers, br, slots, til...]
    ppermute x6 -> x0, starting transfers between devices: 15.7 us -> none  [shifted(): return lax.ppermute(value, axis, pairs)]
    reduce_scatter x3 -> x0, waiting for transfers between devices: 13 us -> none  [the longest x1 6.62 us: local(): lax.psum_scatter(input_rows(combined, d_round, feat_half, lax.axis_size('...]
    all_gather x6 -> x0, blocking collectives: 11.7 us -> none  [the longest x2 3.99 us: local(): lax.all_gather(acts, 'feat', axis=0, tiled=True)]
    unnamed x56 -> x26, local copies, waits for them, and re-layouts: 2.48 us -> 13.7 us
    dot_general x18 -> x0, matrix products: 10.7 us -> none  [the longest x2 1.61 us: local(): jnp.einsum('hf,fn->hn', w_mix[layer], d_out_all, preferred_element_type=j...]
    another operation x9 -> x0, other arithmetic: 6.81 us -> none  [the longest x2 1.42 us: local(): jnp.stack(grads_node)]
  transfers between devices with their start and end apart: 10 -> 0, of which waited for: 7 -> 0; matrix products, arithmetic and copies ran while one was open for 9% -> 0% of each run, Pallas kernels for 0% -> 0%
where the time goes in v1:
time: 53.8 us; the launch traced here: 53 us
  Pallas kernels  37.3 us (69%)
  local copies, waits for them, and re-layouts  15.1 us (28%)
  between operations  0.67 us (1%)
    pallas_call x1, Pallas kernels, local(): pl.pallas_call(functools.partial(kernel, n, reach, layers, br, slots, til...  37.3 us
    unnamed x26, local copies, waits for them, and re-layouts  13.7 us
    pallas_call x2, local copies, waits for them, and re-layouts, local(): pl.pallas_call(functools.partial(kernel, n, reach, layers, br, slots, til...  1.43 us

profile of v1, /device:TPU:0, one launch (start us, length us, event | category | flops | bytes accessed | tf_op | source)
XLA Modules:
  0.0 53.0 jit_solution(1140383029547869534)
XLA Ops:
  0.6 0.9 %copy.19.w_node = bf16[2,128,64]{2,1,0:T(8,128)(2,1)S(1)} copy(bf16[2,128,64]{1,2,0:T(8,128)(2,1)} %param.14) | data formatting | bytes 65536 | tf_op args[1]
  1.5 0.9 %copy.20.w_msg = bf16[2,128,64]{2,1,0:T(8,128)(2,1)S(1)} copy(bf16[2,128,64]{1,2,0:T(8,128)(2,1)} %param.15) | data formatting | bytes 65536 | tf_op args[2]
  2.4 0.9 %copy.21.a_node = bf16[2,128,64]{2,1,0:T(8,128)(2,1)S(1)} copy(bf16[2,128,64]{1,2,0:T(8,128)(2,1)} %param.19) | data formatting | bytes 65536 | tf_op args[6]
  3.3 0.9 %copy.22.a_msg = bf16[2,128,64]{2,1,0:T(8,128)(2,1)S(1)} copy(bf16[2,128,64]{1,2,0:T(8,128)(2,1)} %param.20) | data formatting | bytes 65536 | tf_op args[7]
  4.1 0.0 copy-start
  4.2 1.9 %copy-done = s32[4,12,128,128]{3,2,1,0:T(8,128)S(1)} copy-done((s32[4,12,128,128]{3,2,1,0:T(8,128)S(1)}, s32[4,12,128,128]{3,2,1,0:T(8,128)}, u32[]{:S(2)}) %copy-start) | copy-done | bytes 3145752
  6.0 0.0 copy-start.1
  6.0 0.8 %copy-done.1 = bf16[64,512]{1,0:T(8,128)(2,1)S(1)} copy-done((bf16[64,512]{1,0:T(8,128)(2,1)S(1)}, bf16[64,512]{1,0:T(8,128)(2,1)}, u32[]{:S(2)}) %copy-start.1) | copy-done | bytes 65560
  6.9 0.0 copy-start.2
  6.9 0.8 %copy-done.2 = bf16[64,512]{1,0:T(8,128)(2,1)S(1)} copy-done((bf16[64,512]{1,0:T(8,128)(2,1)S(1)}, bf16[64,512]{1,0:T(8,128)(2,1)}, u32[]{:S(2)}) %copy-start.2) | copy-done | bytes 65560
  7.7 0.0 copy-start.3
  7.7 0.8 %copy-done.3 = bf16[2,64,128]{2,1,0:T(8,128)(2,1)S(1)} copy-done((bf16[2,64,128]{2,1,0:T(8,128)(2,1)S(1)}, bf16[2,64,128]{2,1,0:T(8,128)(2,1)}, u32[]{:S(2)}) %copy-start.3) | copy-done | bytes 32792
  8.5 0.0 copy-start.4
  8.5 0.8 %copy-done.4 = bf16[2,64,128]{2,1,0:T(8,128)(2,1)S(1)} copy-done((bf16[2,64,128]{2,1,0:T(8,128)(2,1)S(1)}, bf16[2,64,128]{2,1,0:T(8,128)(2,1)}, u32[]{:S(2)}) %copy-start.4) | copy-done | bytes 32792
  9.2 0.0 copy-start.5
  9.2 0.7 %copy-done.5 = s32[4,12]{1,0:T(4,128)S(1)} copy-done((s32[4,12]{1,0:T(4,128)S(1)}, s32[4,12]{1,0:T(4,128)}, u32[]{:S(2)}) %copy-start.5) | copy-done | bytes 216
  9.9 0.0 copy-start.6
  9.9 0.7 %copy-done.6 = f32[2,64]{1,0:T(2,128)S(1)} copy-done((f32[2,64]{1,0:T(2,128)S(1)}, f32[2,64]{1,0:T(2,128)}, u32[]{:S(2)}) %copy-start.6) | copy-done | bytes 536
  10.6 0.0 copy-start.7
  10.6 0.7 %copy-done.7 = f32[2,64]{1,0:T(2,128)S(1)} copy-done((f32[2,64]{1,0:T(2,128)S(1)}, f32[2,64]{1,0:T(2,128)}, u32[]{:S(2)}) %copy-start.7) | copy-done | bytes 536
  11.3 0.0 copy-start.8
  11.3 0.7 %copy-done.8 = s32[4]{0:T(128)S(1)} copy-done((s32[4]{0:T(128)S(1)}, s32[4]{0:T(128)}, u32[]{:S(2)}) %copy-start.8) | copy-done | bytes 40
  11.9 37.3 %graph_net.1 = (bf16[64,512]{1,0:T(8,128)(2,1)S(1)}, f32[2,128,64]{2,1,0:T(8,128)S(1)}, f32[2,128,64]{2,1,0:T(8,128)S(1)}, f32[2,64,128]{2,1,0:T(8,128)S(1)}, f32[2,64]{1,0:T(2,128)S(1)}, /*index=5*/f32[2,64]{1,0:T(2,128)S(1)}) custom-call(s32[4,12]{1,0:T(4,128)S(1)} %copy-done.5, s32[4]{0:T(128)S(1)} %copy-done.8, bf16[64,512]{1,0:T(8,128)(2,1)S(1)} %copy-done.1, ...), custom_call_target="tpu_custom_call" | custom-call | tf_op jit(solution)/shard_map/graph_net/pallas_call | solution.py:301
  49.2 0.7 %copy.23 = f32[2,128,64]{1,2,0:T(8,128)} copy(f32[2,128,64]{2,1,0:T(8,128)S(1)} %get-tuple-element.7) | data formatting | bytes 131072 | tf_op jit(solution)/shard_map/graph_net/pallas_call | solution.py:301
  49.9 0.7 %copy.24 = f32[2,128,64]{1,2,0:T(8,128)} copy(f32[2,128,64]{2,1,0:T(8,128)S(1)} %get-tuple-element.8) | data formatting | bytes 131072 | tf_op jit(solution)/shard_map/graph_net/pallas_call | solution.py:301
  50.7 0.6 %copy.29 = bf16[64,512]{1,0:T(8,128)(2,1)} copy(bf16[64,512]{1,0:T(8,128)(2,1)S(1)} %get-tuple-element.18) | data formatting | bytes 131072
  51.3 0.6 %copy.30 = f32[2,64,128]{2,1,0:T(8,128)} copy(f32[2,64,128]{2,1,0:T(8,128)S(1)} %get-tuple-element.21) | data formatting | bytes 131072
  51.9 0.6 %copy.31 = f32[2,64]{1,0:T(2,128)} copy(f32[2,64]{1,0:T(2,128)S(1)} %get-tuple-element.22) | data formatting | bytes 1024
  52.5 0.6 %copy.32 = f32[2,64]{1,0:T(2,128)} copy(f32[2,64]{1,0:T(2,128)S(1)} %get-tuple-element.23) | data formatting | bytes 1024
Async XLA Ops:
  4.1 1.9 %copy-start = (s32[4,12,128,128]{3,2,1,0:T(8,128)S(1)}, s32[4,12,128,128]{3,2,1,0:T(8,128)}, u32[]{:S(2)}) copy-start(s32[4,12,128,128]{3,2,1,0:T(8,128)} %masks.1) | copy-start | bytes 9437188
  6.0 0.8 %copy-start.1 = (bf16[64,512]{1,0:T(8,128)(2,1)S(1)}, bf16[64,512]{1,0:T(8,128)(2,1)}, u32[]{:S(2)}) copy-start(bf16[64,512]{1,0:T(8,128)(2,1)} %feats.1) | copy-start | bytes 196612
  6.9 0.8 %copy-start.2 = (bf16[64,512]{1,0:T(8,128)(2,1)S(1)}, bf16[64,512]{1,0:T(8,128)(2,1)}, u32[]{:S(2)}) copy-start(bf16[64,512]{1,0:T(8,128)(2,1)} %cot.1) | copy-start | bytes 196612
  7.7 0.8 %copy-start.3 = (bf16[2,64,128]{2,1,0:T(8,128)(2,1)S(1)}, bf16[2,64,128]{2,1,0:T(8,128)(2,1)}, u32[]{:S(2)}) copy-start(bf16[2,64,128]{2,1,0:T(8,128)(2,1)} %w_mix.1) | copy-start | bytes 98308
  8.5 0.8 %copy-start.4 = (bf16[2,64,128]{2,1,0:T(8,128)(2,1)S(1)}, bf16[2,64,128]{2,1,0:T(8,128)(2,1)}, u32[]{:S(2)}) copy-start(bf16[2,64,128]{2,1,0:T(8,128)(2,1)} %a_mix.1) | copy-start | bytes 98308
  9.2 0.7 %copy-start.5 = (s32[4,12]{1,0:T(4,128)S(1)}, s32[4,12]{1,0:T(4,128)}, u32[]{:S(2)}) copy-start(s32[4,12]{1,0:T(4,128)} %cols.1) | copy-start | bytes 580
  9.9 0.7 %copy-start.6 = (f32[2,64]{1,0:T(2,128)S(1)}, f32[2,64]{1,0:T(2,128)}, u32[]{:S(2)}) copy-start(f32[2,64]{1,0:T(2,128)} %hbias.1) | copy-start | bytes 1540
  10.6 0.7 %copy-start.7 = (f32[2,64]{1,0:T(2,128)S(1)}, f32[2,64]{1,0:T(2,128)}, u32[]{:S(2)}) copy-start(f32[2,64]{1,0:T(2,128)} %obias.1) | copy-start | bytes 1540
  11.3 0.7 %copy-start.8 = (s32[4]{0:T(128)S(1)}, s32[4]{0:T(128)}, u32[]{:S(2)}) copy-start(s32[4]{0:T(128)} %count.1) | copy-start | bytes 52

commit v2 on v1

--- a/solution.py
+++ b/solution.py
@@ -38,11 +38,11 @@
 
 def kernel(
     n, reach, layers, br, slots, tile, half, nodes,
-    cols, count, feats, w_node, w_msg, w_mix, hbias, obias, a_node, a_msg, a_mix, cot, masks,
-    out_x, g_node, g_msg, g_mix, g_hb, g_ob,
-    mask_v, mask_b, adj, xwin, xm, wt, wmix, wmixt, wback, bias, dy, pre_s, hid, dr, dh, part_out, part_in,
-    gbuf, grecv, gred,
-    s_mask, s_xs, s_xr, s_ps, s_pr, s_fs, s_fr, s_gs, s_gr, s_as, s_ar,
+    cols, count, feats, w_node, w_msg, w_mix, hbias, obias, cot, masks,
+    out_x, gred,
+    cols_s, count_s, hb_v, ob_v, mask_v, mask_b, adj, xwin, xm, wt, wmix, wmixt, wback, bias, dy, pre_s, hid, dr, dh, part_out, part_in,
+    gbuf, grecv,
+    s_in, s_mask, s_xs, s_xr, s_ps, s_pr, s_fs, s_fr, s_gs, s_gr, s_as, s_ar,
 ):
     feat = 2 * half
     me = lax.axis_index("blk")
@@ -62,21 +62,29 @@
     for step in range(1, n):
         pl.semaphore_signal(barrier, inc=1, device_id={"blk": at(step)}, device_id_type=MESH)
 
+    moves = [
+        (cols, cols_s),
+        (count, count_s),
+        (hbias, hb_v),
+        (obias, ob_v),
+        (feats, xm.at[0, own]),
+        (feats, xwin.at[0, reach]),
+        (cot, dy.at[layers - 1, own]),
+        (w_node, wt.at[:, own, 0:feat]),
+        (w_msg, wt.at[:, own, feat : 2 * feat]),
+        (w_mix, wmix.at[:, own]),
+    ]
+    loads = [pltpu.make_async_copy(src, dst, s_in.at[i]) for i, (src, dst) in enumerate(moves)]
+    for copy in loads[0:4]:
+        copy.start()
     mask_copies = [pltpu.make_async_copy(masks.at[r], mask_v.at[r], s_mask.at[r]) for r in range(br)]
-    for copy in mask_copies:
+    for copy in loads[4:] + mask_copies:
         copy.start()
-
-    xm[0, own] = feats[...]
-    xwin[0, reach] = feats[...]
-    dy[layers - 1, own] = cot[...]
-    unit = jnp.where(eye(half), 1.0, 0.0).astype(BF16)
-    for l in range(layers):
-        wt[l, own, 0:feat] = mm_nt(unit, w_node[l]).astype(BF16)
-        wt[l, own, feat : 2 * feat] = mm_nt(unit, w_msg[l]).astype(BF16)
-        wmix[l, own] = w_mix[l]
+    for copy in loads[0:4]:
+        copy.wait()
     bias[side] = jnp.zeros(bias.shape[1:], F32)
-    bias[side, 0:layers, 0:half] = hbias[...]
-    bias[side, layers : 2 * layers, 0:half] = obias[...]
+    bias[side, 0:layers, 0:half] = hb_v[...]
+    bias[side, layers : 2 * layers, 0:half] = ob_v[...]
 
     pl.semaphore_wait(barrier, n)
 
@@ -105,11 +113,12 @@
 
     arriving = spread_out(feats, 0)
     first = [
-        to_peer(0, wmix.at[:, own], wmix.at[:, own]),
-        to_peer(1, wt.at[:, own], wt.at[:, own]),
-        to_peer(2, bias.at[side], bias.at[side]),
-        to_peer(3, dy.at[layers - 1, own], dy.at[layers - 1, own]),
-        to_peer(4, xm.at[0, own], xm.at[0, own]),
+        to_peer(0, w_mix, wmix.at[:, own]),
+        to_peer(1, w_node, wt.at[:, own, 0:feat]),
+        to_peer(2, w_msg, wt.at[:, own, feat : 2 * feat]),
+        to_peer(3, bias.at[side], bias.at[side]),
+        to_peer(4, cot, dy.at[layers - 1, own]),
+        to_peer(5, feats, xm.at[0, own]),
     ]
 
     for r in range(br):
@@ -118,10 +127,10 @@
     def build_row(r, unused):
         for k in range(slots):
             mask_b[k] = mask_v[r, k].astype(F32).astype(BF16)
-        live = count[r]
+        live = count_s[r]
         targets = []
         for k in range(slots):
-            name = cols[r, k]
+            name = cols_s[r, k]
             block = lax.rem(lax.div(name, br) - me + reach + n, n) * br + lax.rem(name, br)
             targets.append(jnp.where(k < live, block, -1))
 
@@ -144,7 +153,9 @@
         degree = degree + mm_nt(ones, adj[j])
     inverse = 1.0 / (degree[0:1] + 1.0)
 
-    for copy in first[0:4]:
+    for copy in loads[4:]:
+        copy.wait()
+    for copy in first[0:5]:
         copy.wait_recv()
     unit_f = jnp.where(eye(feat), 1.0, 0.0).astype(BF16)
     hb, ob = [], []
@@ -158,7 +169,7 @@
         )
         ob.append([to_column(bias[s, layers + l : layers + l + 1, 0:half]) for s in (side, peer)])
     dh[...] = mm(wmix[layers - 1], dy[layers - 1])
-    first[4].wait_recv()
+    first[5].wait_recv()
 
     for l in range(layers):
         summed = mm_nt(xwin[l, reach], adj[reach])
@@ -167,7 +178,7 @@
             summed = summed + mm_nt(xwin[l, slot], adj[slot])
         message = (xm[l, own].astype(F32) + summed) * inverse
         xm[l, own_msg] = message.astype(BF16)
-        copy = to_peer(5 + l, xm.at[l, own_msg], xm.at[l, own_msg])
+        copy = to_peer(6 + l, xm.at[l, own_msg], xm.at[l, own_msg])
         part = mm(wt[l, :, 0:feat], xm[l, 0:feat]) + hb[l]
         copy.wait_recv()
         pre = part + mm(wt[l, :, feat : 2 * feat], xm[l, feat : 2 * feat])
@@ -203,31 +214,14 @@
             for step in range(1, n)
         ]
 
-    def finish(l, copies):
-        for copy in copies:
-            copy.wait_recv()
-        per = feat // chunk
-        both = gred[l, 0:per].reshape(feat, 2 * half)
-        g_node[l] = both[:, 0:half] + (w_node[l].astype(F32) - a_node[l].astype(F32))
-        g_msg[l] = both[:, half : 2 * half] + (w_msg[l].astype(F32) - a_msg[l].astype(F32))
-        more = half // chunk
-        mixed = gred[l, per : per + more].reshape(half, feat)
-        g_mix[l] = mixed + (w_mix[l].astype(F32) - a_mix[l].astype(F32))
-        g_hb[l : l + 1] = gred[l, per + more, 0:1, 0:half]
-        g_ob[l : l + 1] = gred[l, per + more, 1:2, 0:half]
-
     def gradients(l, d_own, d_round_own, dy_own):
-        zero = jnp.zeros((half, nodes), BF16)
-        both = mm_nt(xm[l, 0:feat], jnp.concatenate([d_round_own, zero], axis=0)) + mm_nt(
-            xm[l, feat : 2 * feat], jnp.concatenate([zero, d_round_own], axis=0)
-        )
-        per = feat // chunk
-        more = half // chunk
-        gbuf[l, 0:per] = both.reshape(per, chunk, 2 * half)
-        gbuf[l, per : per + more] = mm_nt(hid[l, own], dy[l]).reshape(more, chunk, feat)
-        gbuf[l, per + more :] = jnp.zeros((n - per - more, chunk, 2 * half), F32)
-        gbuf[l, per + more, 0:1, 0:half] = to_row(jnp.sum(d_own, axis=1, keepdims=True))
-        gbuf[l, per + more, 1:2, 0:half] = to_row(jnp.sum(dy_own, axis=1, keepdims=True))
+        per = half // chunk
+        gbuf[l, 0:per] = mm_nt(d_round_own, xm[l, 0:feat]).reshape(per, chunk, feat)
+        gbuf[l, per : 2 * per] = mm_nt(d_round_own, xm[l, feat : 2 * feat]).reshape(per, chunk, feat)
+        gbuf[l, 2 * per : 3 * per] = mm_nt(hid[l, own], dy[l]).reshape(per, chunk, feat)
+        gbuf[l, 3 * per :] = jnp.zeros((n - 3 * per, chunk, feat), F32)
+        gbuf[l, 3 * per, 0:1, 0:half] = to_row(jnp.sum(d_own, axis=1, keepdims=True))
+        gbuf[l, 3 * per, 1:2, 0:half] = to_row(jnp.sum(dy_own, axis=1, keepdims=True))
 
     reducing = {}
     for l in range(layers - 1, -1, -1):
@@ -268,7 +262,7 @@
                 copy.wait_recv()
                 before = before + part_in[l - 1, landing].astype(F32)
             dy[l - 1, own] = before.astype(BF16)
-            copy = to_peer(5 + layers + l, dy.at[l - 1, own], dy.at[l - 1, own])
+            copy = to_peer(6 + layers + l, dy.at[l - 1, own], dy.at[l - 1, own])
             copy.wait_recv()
         else:
             d_own = mm(wmix[l, own], dy[l]) * pre_s[l, own]
@@ -278,9 +272,45 @@
     for l in range(layers - 1, -1, -1):
         sharing[l] = reduce_end(l, reducing[l])
     for l in range(layers - 1, -1, -1):
-        finish(l, sharing[l])
+        for copy in sharing[l]:
+            copy.wait_recv()
     for copy in pending:
         copy.wait_send()
+
+
+def finish(x_in, gred, w_node, w_msg, w_mix, a_node, a_msg, a_mix, out_x, g_node, g_msg, g_mix, g_hb, g_ob,
+           wv, o_node, o_msg, o_mix, o_hb, o_ob, s_in, s_out):
+    layers, half, feat = w_node.shape
+    chunk = gred.shape[2]
+    per = half // chunk
+    loads = [
+        pltpu.make_async_copy(src, wv.at[i], s_in.at[i])
+        for i, src in enumerate((w_node, a_node, w_msg, a_msg, w_mix, a_mix))
+    ]
+    for copy in loads:
+        copy.start()
+    stores = [pltpu.make_async_copy(x_in, out_x, s_out.at[0])]
+    stores[0].start()
+
+    def leave(src, dst):
+        copy = pltpu.make_async_copy(src, dst, s_out.at[len(stores)])
+        copy.start()
+        stores.append(copy)
+
+    for l in range(layers):
+        o_hb[l : l + 1] = gred[l, 3 * per, 0:1, 0:half]
+        o_ob[l : l + 1] = gred[l, 3 * per, 1:2, 0:half]
+    leave(o_hb, g_hb)
+    leave(o_ob, g_ob)
+    for i, (held, dst) in enumerate(((o_node, g_node), (o_msg, g_msg), (o_mix, g_mix))):
+        loads[2 * i].wait()
+        loads[2 * i + 1].wait()
+        for l in range(layers):
+            total = gred[l, i * per : (i + 1) * per].reshape(half, feat)
+            held[l] = total + (wv[2 * i, l].astype(F32) - wv[2 * i + 1, l].astype(F32))
+        leave(held, dst)
+    for copy in stores:
+        copy.wait()
 
 
 def local(
@@ -297,20 +327,23 @@
     chunk = max(8, 256 // n)
     dma = pltpu.SemaphoreType.DMA
     vmem = pl.BlockSpec(memory_space=pltpu.VMEM)
-    smem = pl.BlockSpec(memory_space=pltpu.SMEM)
-    return pl.pallas_call(
+    hbm = pl.BlockSpec(memory_space=pltpu.HBM)
+    w_node, w_msg, anchor_node, anchor_msg = (
+        jnp.swapaxes(value, 1, 2) for value in (w_node, w_msg, anchor_node, anchor_msg)
+    )
+    last, sums = pl.pallas_call(
         functools.partial(kernel, n, reach, layers, br, slots, tile, half, nodes),
         out_shape=(
             jax.ShapeDtypeStruct((half, nodes), BF16),
-            jax.ShapeDtypeStruct((layers, feat, half), F32),
-            jax.ShapeDtypeStruct((layers, feat, half), F32),
-            jax.ShapeDtypeStruct((layers, half, feat), F32),
-            jax.ShapeDtypeStruct((layers, half), F32),
-            jax.ShapeDtypeStruct((layers, half), F32),
+            jax.ShapeDtypeStruct((layers, n, chunk, feat), F32),
         ),
-        in_specs=[smem, smem] + [vmem] * 10 + [pl.BlockSpec(memory_space=pl.ANY)],
-        out_specs=(vmem,) * 6,
+        in_specs=[hbm] * 10,
+        out_specs=(vmem,) * 2,
         scratch_shapes=[
+            pltpu.SMEM((br, slots), jnp.int32),
+            pltpu.SMEM((br,), jnp.int32),
+            pltpu.VMEM((layers, half), F32),
+            pltpu.VMEM((layers, half), F32),
             pltpu.VMEM((br, slots, tile, tile), jnp.int32),
             pltpu.VMEM((slots, tile, tile), BF16),
             pltpu.VMEM((wins, nodes, nodes), BF16),
@@ -330,27 +363,50 @@
             pltpu.VMEM((layers - 1, wins, half, nodes), BF16),
             pltpu.VMEM((layers, n, chunk, feat), F32),
             pltpu.VMEM((layers, n - 1, chunk, feat), F32),
-            pltpu.VMEM((layers, n, chunk, feat), F32),
+            dma((10,)),
             dma((br,)),
             dma((layers, wins)),
             dma((layers, wins)),
             dma((layers - 1, wins)),
             dma((layers - 1, wins)),
-            dma((5 + 2 * layers + 1,)),
-            dma((5 + 2 * layers + 1,)),
+            dma((6 + 2 * layers,)),
+            dma((6 + 2 * layers,)),
             dma((layers, n - 1)),
             dma((layers, n - 1)),
             dma((layers, n - 1)),
             dma((layers, n - 1)),
         ],
         compiler_params=pltpu.CompilerParams(
-            collective_id=0, has_side_effects=True, vmem_limit_bytes=50 * 1024 * 1024
+            collective_id=0, has_side_effects=True, vmem_limit_bytes=56 * 1024 * 1024
         ),
         name="graph_net",
-    )(
-        tile_cols, tile_count, features, w_node, w_msg, w_mix, hbias, obias,
-        anchor_node, anchor_msg, anchor_mix, cotangent, tile_masks,
-    )
+    )(tile_cols, tile_count, features, w_node, w_msg, w_mix, hbias, obias, cotangent, tile_masks)
+    square = (layers, half, feat)
+    out, g_node, g_msg, g_mix, g_hb, g_ob = pl.pallas_call(
+        finish,
+        out_shape=(
+            jax.ShapeDtypeStruct((half, nodes), BF16),
+            jax.ShapeDtypeStruct(square, F32),
+            jax.ShapeDtypeStruct(square, F32),
+            jax.ShapeDtypeStruct(square, F32),
+            jax.ShapeDtypeStruct((layers, half), F32),
+            jax.ShapeDtypeStruct((layers, half), F32),
+        ),
+        in_specs=[vmem] * 2 + [hbm] * 6,
+        out_specs=(hbm,) * 6,
+        scratch_shapes=[
+            pltpu.VMEM((6,) + square, BF16),
+            pltpu.VMEM(square, F32),
+            pltpu.VMEM(square, F32),
+            pltpu.VMEM(square, F32),
+            pltpu.VMEM((layers, half), F32),
+            pltpu.VMEM((layers, half), F32),
+            dma((6,)),
+            dma((6,)),
+        ],
+        name="finish",
+    )(last, sums, w_node, w_msg, w_mix, anchor_node, anchor_msg, anchor_mix)
+    return out, jnp.swapaxes(g_node, 1, 2), jnp.swapaxes(g_msg, 1, 2), g_mix, g_hb, g_ob
 
 
 def solution(mesh):

time: 53.8 us -> 40.9 us (0.76); the launches traced: 53 us -> 40.7 us
  local copies, waits for them, and re-layouts: 15.1 us -> 0 us
  Pallas kernels: 37.3 us -> 40 us
    unnamed x26 -> x0, local copies, waits for them, and re-layouts: 13.7 us -> none
    pallas_call x0 -> x1, Pallas kernels: none -> 2.6 us  [local(): pl.pallas_call(finish, out_shape=(jax.ShapeDtypeStruct((half, nodes), BF1...]
    pallas_call x2 -> x0, local copies, waits for them, and re-layouts: 1.43 us -> none  [local(): pl.pallas_call(functools.partial(kernel, n, reach, layers, br, slots, til...]
where the time goes in v2:
time: 40.9 us; the launch traced here: 40.7 us
  Pallas kernels  40 us (98%)
  between operations  0.64 us (2%)
    pallas_call x1, Pallas kernels, local(): pl.pallas_call(functools.partial(kernel, n, reach, layers, br, slots, til...  37.4 us
    pallas_call x1, Pallas kernels, local(): pl.pallas_call(finish, out_shape=(jax.ShapeDtypeStruct((half, nodes), BF1...  2.6 us

profile of v2, /device:TPU:0, one launch (start us, length us, event | category | flops | bytes accessed | tf_op | source)
XLA Modules:
  0.0 40.7 jit_solution(2784461201417941984)
XLA Ops:
  0.6 37.4 %graph_net.1 = (bf16[64,512]{1,0:T(8,128)(2,1)}, f32[2,8,32,128]{3,2,1,0:T(8,128)}) custom-call(s32[4,12]{1,0:T(4,128)} %cols.1, s32[4]{0:T(128)} %count.1, bf16[64,512]{1,0:T(8,128)(2,1)} %feats.1, bf16[2,64,128]{2,1,0:T(8,128)(2,1)} %bitcast.6, bf16[2,64,128]{2,1,0:T(8,128)(2,1)} %bitcast.8, bf16[2,64,128]{2,1,0:T(8,128)(2,1)} %w_mix.3, f32[2,64]{1,0:T(2,128)} %hbias.1, ...), custom_call_target="tpu_custom_call" | custom-call | tf_op jit(solution)/shard_map/graph_net/pallas_call | solution.py:334
  38.1 2.6 %finish.1 = (bf16[64,512]{1,0:T(8,128)(2,1)}, f32[2,64,128]{2,1,0:T(8,128)}, f32[2,64,128]{2,1,0:T(8,128)}, f32[2,64,128]{2,1,0:T(8,128)}, f32[2,64]{1,0:T(2,128)}, /*index=5*/f32[2,64]{1,0:T(2,128)}) custom-call(bf16[64,512]{1,0:T(8,128)(2,1)} %get-tuple-element.14.x_in, f32[2,8,32,128]{3,2,1,0:T(8,128)} %get-tuple-element.15.gred, ...), custom_call_target="tpu_custom_call" | custom-call | tf_op jit(solution)/shard_map/finish/pallas_call | solution.py:385

commit v3 on v2

--- a/solution.py
+++ b/solution.py
@@ -41,7 +41,7 @@
     cols, count, feats, w_node, w_msg, w_mix, hbias, obias, cot, masks,
     out_x, gred,
     cols_s, count_s, hb_v, ob_v, mask_v, mask_b, adj, xwin, xm, wt, wmix, wmixt, wback, bias, dy, pre_s, hid, dr, dh, part_out, part_in,
-    gbuf, grecv,
+    gbuf, grecv, bias_s,
     s_in, s_mask, s_xs, s_xr, s_ps, s_pr, s_fs, s_fr, s_gs, s_gr, s_as, s_ar,
 ):
     feat = 2 * half
@@ -204,11 +204,18 @@
         return copies
 
     def reduce_end(l, copies):
-        total = gbuf[l, me]
+        total = gbuf[l, me].astype(F32)
         for step in range(1, n):
             copies[step - 1].wait_recv()
-            total = total + grecv[l, step - 1]
-        gred[l, me] = total
+            total = total + grecv[l, step - 1].astype(F32)
+        low = jnp.concatenate([total[2:4], jnp.zeros((chunk - 2, feat), F32)], axis=0)
+        row = lax.broadcasted_iota(jnp.int32, (chunk, feat), 0)
+        pair = total + low
+        high = pair.astype(BF16).astype(F32)
+        rest = jnp.concatenate([jnp.zeros((2, feat), F32), (pair - high)[0 : chunk - 2]], axis=0)
+        split = jnp.where(row < 2, high, rest)
+        slot = lax.broadcasted_iota(jnp.int32, (chunk, feat), 0) * 0 + me
+        gred[l, me] = jnp.where(slot == 3 * (half // chunk), split, total).astype(BF16)
         return [
             send(gred.at[l, me], gred.at[l, me], s_as.at[l, step - 1], s_ar.at[l, step - 1], {"blk": at(step)})
             for step in range(1, n)
@@ -216,12 +223,25 @@
 
     def gradients(l, d_own, d_round_own, dy_own):
         per = half // chunk
-        gbuf[l, 0:per] = mm_nt(d_round_own, xm[l, 0:feat]).reshape(per, chunk, feat)
-        gbuf[l, per : 2 * per] = mm_nt(d_round_own, xm[l, feat : 2 * feat]).reshape(per, chunk, feat)
-        gbuf[l, 2 * per : 3 * per] = mm_nt(hid[l, own], dy[l]).reshape(per, chunk, feat)
-        gbuf[l, 3 * per :] = jnp.zeros((n - 3 * per, chunk, feat), F32)
-        gbuf[l, 3 * per, 0:1, 0:half] = to_row(jnp.sum(d_own, axis=1, keepdims=True))
-        gbuf[l, 3 * per, 1:2, 0:half] = to_row(jnp.sum(dy_own, axis=1, keepdims=True))
+        gbuf[l, 0:per] = mm_nt(d_round_own, xm[l, 0:feat]).reshape(per, chunk, feat).astype(BF16)
+        gbuf[l, per : 2 * per] = (
+            mm_nt(d_round_own, xm[l, feat : 2 * feat]).reshape(per, chunk, feat).astype(BF16)
+        )
+        gbuf[l, 2 * per : 3 * per] = mm_nt(hid[l, own], dy[l]).reshape(per, chunk, feat).astype(BF16)
+        if n > 3 * per + 1:
+            gbuf[l, 3 * per + 1 :] = jnp.zeros((n - 3 * per - 1, chunk, feat), BF16)
+        sums = jnp.concatenate(
+            [
+                to_row(jnp.sum(d_own, axis=1, keepdims=True)),
+                to_row(jnp.sum(dy_own, axis=1, keepdims=True)),
+            ],
+            axis=0,
+        )
+        high = sums.astype(BF16).astype(F32)
+        bias_s[...] = jnp.zeros(bias_s.shape, F32)
+        bias_s[0:2, 0:half] = high
+        bias_s[2:4, 0:half] = sums - high
+        gbuf[l, 3 * per] = bias_s[...].astype(BF16)
 
     reducing = {}
     for l in range(layers - 1, -1, -1):
@@ -257,12 +277,12 @@
                 last = xm[l, own].astype(F32) + mm(wmixt[l, own], hid[l]) + ob[l][0]
                 out_x[...] = last.astype(BF16)
             gradients(l, dh[own], dr[own], dy_own)
-            reducing[l] = reduce_start(l)
             for landing, copy in incoming:
                 copy.wait_recv()
                 before = before + part_in[l - 1, landing].astype(F32)
             dy[l - 1, own] = before.astype(BF16)
             copy = to_peer(6 + layers + l, dy.at[l - 1, own], dy.at[l - 1, own])
+            reducing[l] = reduce_start(l)
             copy.wait_recv()
         else:
             d_own = mm(wmix[l, own], dy[l]) * pre_s[l, own]
@@ -298,15 +318,16 @@
         stores.append(copy)
 
     for l in range(layers):
-        o_hb[l : l + 1] = gred[l, 3 * per, 0:1, 0:half]
-        o_ob[l : l + 1] = gred[l, 3 * per, 1:2, 0:half]
+        pair = gred[l, 3 * per].astype(F32)
+        o_hb[l : l + 1] = pair[0:1, 0:half] + pair[2:3, 0:half]
+        o_ob[l : l + 1] = pair[1:2, 0:half] + pair[3:4, 0:half]
     leave(o_hb, g_hb)
     leave(o_ob, g_ob)
     for i, (held, dst) in enumerate(((o_node, g_node), (o_msg, g_msg), (o_mix, g_mix))):
         loads[2 * i].wait()
         loads[2 * i + 1].wait()
         for l in range(layers):
-            total = gred[l, i * per : (i + 1) * per].reshape(half, feat)
+            total = gred[l, i * per : (i + 1) * per].astype(F32).reshape(half, feat)
             held[l] = total + (wv[2 * i, l].astype(F32) - wv[2 * i + 1, l].astype(F32))
         leave(held, dst)
     for copy in stores:
@@ -324,7 +345,7 @@
     n = lax.axis_size("blk")
     reach = max(1, n // 8)
     wins = 2 * reach + 1
-    chunk = max(8, 256 // n)
+    chunk = max(16, 256 // n)
     dma = pltpu.SemaphoreType.DMA
     vmem = pl.BlockSpec(memory_space=pltpu.VMEM)
     hbm = pl.BlockSpec(memory_space=pltpu.HBM)
@@ -335,7 +356,7 @@
         functools.partial(kernel, n, reach, layers, br, slots, tile, half, nodes),
         out_shape=(
             jax.ShapeDtypeStruct((half, nodes), BF16),
-            jax.ShapeDtypeStruct((layers, n, chunk, feat), F32),
+            jax.ShapeDtypeStruct((layers, n, chunk, feat), BF16),
         ),
         in_specs=[hbm] * 10,
         out_specs=(vmem,) * 2,
@@ -361,8 +382,9 @@
             pltpu.VMEM((feat, nodes), F32),
             pltpu.VMEM((layers - 1, wins, half, nodes), BF16),
             pltpu.VMEM((layers - 1, wins, half, nodes), BF16),
-            pltpu.VMEM((layers, n, chunk, feat), F32),
-            pltpu.VMEM((layers, n - 1, chunk, feat), F32),
+            pltpu.VMEM((layers, n, chunk, feat), BF16),
+            pltpu.VMEM((layers, n - 1, chunk, feat), BF16),
+            pltpu.VMEM((chunk, feat), F32),
             dma((10,)),
             dma((br,)),
             dma((layers, wins)),

time: 40.9 us -> 38.8 us (0.949)
  Pallas kernels: 40 us -> 37.9 us
    pallas_call x1, Pallas kernels: 37.4 us -> 35.4 us  [local(): pl.pallas_call(functools.partial(kernel, n, reach, layers, br, slots, til...]
where the time goes in v3:
time: 38.8 us; the launch traced here: 38.6 us
  Pallas kernels  37.9 us (98%)
  between operations  0.64 us (2%)
    pallas_call x1, Pallas kernels, local(): pl.pallas_call(functools.partial(kernel, n, reach, layers, br, slots, til...  35.4 us
    pallas_call x1, Pallas kernels, local(): pl.pallas_call(finish, out_shape=(jax.ShapeDtypeStruct((half, nodes), BF1...  2.56 us

profile of v3, /device:TPU:0, one launch (start us, length us, event | category | flops | bytes accessed | tf_op | source)
XLA Modules:
  0.0 38.6 jit_solution(5859591622761916609)
XLA Ops:
  0.6 35.4 %graph_net.1 = (bf16[64,512]{1,0:T(8,128)(2,1)}, bf16[2,8,32,128]{3,2,1,0:T(8,128)(2,1)}) custom-call(s32[4,12]{1,0:T(4,128)} %cols.1, s32[4]{0:T(128)} %count.1, bf16[64,512]{1,0:T(8,128)(2,1)} %feats.1, bf16[2,64,128]{2,1,0:T(8,128)(2,1)} %bitcast.6, bf16[2,64,128]{2,1,0:T(8,128)(2,1)} %bitcast.8, bf16[2,64,128]{2,1,0:T(8,128)(2,1)} %w_mix.3, ...), custom_call_target="tpu_custom_call" | custom-call | tf_op jit(solution)/shard_map/graph_net/pallas_call | solution.py:355
  36.0 2.6 %finish.1 = (bf16[64,512]{1,0:T(8,128)(2,1)}, f32[2,64,128]{2,1,0:T(8,128)}, f32[2,64,128]{2,1,0:T(8,128)}, f32[2,64,128]{2,1,0:T(8,128)}, f32[2,64]{1,0:T(2,128)}, /*index=5*/f32[2,64]{1,0:T(2,128)}) custom-call(bf16[64,512]{1,0:T(8,128)(2,1)} %get-tuple-element.14.x_in, bf16[2,8,32,128]{3,2,1,0:T(8,128)(2,1)} %get-tuple-element.15.gred, ...), custom_call_target="tpu_custom_call" | custom-call | tf_op jit(solution)/shard_map/finish/pallas_call | solution.py:407
